TPU v7x, 512 devices: a whole 4x4x16 slice. The times are simulated.
512 devices in a mesh: blk: 64 (over z, x), uly: 8 (over y, core).
Axes of the slice: x: 4, y: 4, z: 16, core: 2. Of those that a mesh axis runs over, the one named last changes fastest.
Arguments:
- queries: bfloat16 [65536, 8192], P(('blk', 'uly'))
- keys: bfloat16 [65536, 1024], P(('blk', 'uly'))
- values: bfloat16 [65536, 1024], P(('blk', 'uly')), may hold values from -6 to 6
- chosen: int32 [128, 8, 2], replicated, may hold values from 0 to 126, as said below
Outputs:
- attended: bfloat16 [65536, 8192], P(('blk', 'uly'))
Inputs may be any that keep to these rules, and one draw needn't show every extreme that they name: For attention block j and key-value head h, chosen[j, h, 0] and chosen[j, h, 1] differ; for j >= 2 both are below j; for j < 2 at least one is not below j. An id that is not below j selects nothing.
All inputs are finite; a program needn't handle non-finite values.
Results may differ from a plain program's by a relative error of at most 0.0046.
Values may be sent and summed in bfloat16 or wider, within the bound.
A program may use at most 64 MiB of HBM per device.

v0:
```python
import jax
import jax.numpy as jnp
from jax import lax
from jax.sharding import PartitionSpec as P

BS = 512
HD = 128
GROUP = 8


def as_sent(x):
    return jax.tree.map(lambda a: a.astype(jnp.bfloat16) if a.dtype == jnp.float32 else a, x)


def local(queries, keys, values, chosen):
    scale = HD ** (-0.5)
    blk_count = lax.axis_size("blk")
    rank = lax.axis_index("blk")
    head = lax.axis_index("uly")
    tok = queries.shape[0]
    kv_heads = keys.shape[1] // HD
    q_split = queries.reshape(tok, kv_heads, GROUP * HD)
    kv_split = jnp.concatenate(
        [keys.reshape(tok, kv_heads, HD), values.reshape(tok, kv_heads, HD)], axis=2
    )
    q_head, kv_head = (
        lax.all_to_all(q_split, "uly", split_axis=1, concat_axis=0, tiled=True),
        lax.all_to_all(kv_split, "uly", split_axis=1, concat_axis=0, tiled=True),
    )
    span = q_head.shape[0]
    blocks_here = span // BS
    pieces = BS // blk_count
    spread = lax.all_to_all(
        kv_head.reshape(1, blocks_here, blk_count, pieces, 2 * HD),
        "blk",
        split_axis=2,
        concat_axis=0,
        tiled=True,
    )
    table = spread.reshape(blk_count * blocks_here, pieces, 2 * HD)
    wanted = lax.dynamic_index_in_dim(chosen, head, 1, keepdims=False)
    own_ids = lax.dynamic_slice_in_dim(wanted, rank * blocks_here, blocks_here, 0)
    block_ids = rank * blocks_here + jnp.arange(blocks_here, dtype=jnp.int32)
    usable = own_ids < block_ids[:, None]
    q_blocks = q_head.reshape(blocks_here, BS, GROUP, HD)
    own_rows = kv_head.reshape(blocks_here, BS, 2 * HD)
    causal = jnp.arange(BS, dtype=jnp.int32)[None, :] <= jnp.arange(BS, dtype=jnp.int32)[:, None]
    items = jnp.arange(blocks_here * GROUP, dtype=jnp.int32)
    contract = (((1,), (1,)), ((), ()))

    def query_of(item):
        block_q = lax.dynamic_index_in_dim(q_blocks, item // GROUP, 0, keepdims=False)
        return lax.dynamic_index_in_dim(block_q, item % GROUP, 1, keepdims=False)

    def own_part(item):
        query_rows = query_of(item)
        kv_rows = lax.dynamic_index_in_dim(own_rows, item // GROUP, 0, keepdims=False)
        scores = (
            lax.dot_general(
                query_rows, kv_rows[:, :HD], contract, preferred_element_type=jnp.float32
            )
            * scale
        )
        return jnp.where(causal, scores, -jnp.inf)

    def finish(item, own_scores, picked):
        index = item // GROUP
        query_rows = query_of(item)
        own_kv = lax.dynamic_index_in_dim(own_rows, index, 0, keepdims=False)
        routed_kv = lax.dynamic_index_in_dim(picked, index, 0, keepdims=False)
        allowed = lax.dynamic_index_in_dim(usable, index, 0, keepdims=False)
        routed_scores = (
            lax.dot_general(
                query_rows, routed_kv[:, :HD], contract, preferred_element_type=jnp.float32
            )
            * scale
        )
        routed_mask = jnp.repeat(allowed, BS, total_repeat_length=2 * BS)[None, :]
        routed_scores = jnp.where(routed_mask, routed_scores, -jnp.inf)
        top = jnp.maximum(jnp.max(own_scores, axis=-1), jnp.max(routed_scores, axis=-1))[:, None]
        own_weights = jnp.exp(own_scores - top)
        routed_weights = jnp.exp(routed_scores - top)
        total = jnp.sum(own_weights, axis=-1) + jnp.sum(routed_weights, axis=-1)
        summed = jnp.dot(
            own_weights.astype(jnp.bfloat16), own_kv[:, HD:], preferred_element_type=jnp.float32
        )
        summed = summed + jnp.dot(
            routed_weights.astype(jnp.bfloat16),
            routed_kv[:, HD:],
            preferred_element_type=jnp.float32,
        )
        return (summed / total[:, None]).astype(jnp.bfloat16)

    request = table[wanted.reshape(-1)].reshape(blk_count, blocks_here * 2, 1, pieces, 2 * HD)
    arrived = lax.all_to_all(request, "blk", split_axis=0, concat_axis=2, tiled=True)
    picked = arrived.reshape(blocks_here, 2 * BS, 2 * HD)

    def with_late(item):
        return finish(item, own_part(item), picked)

    result = lax.map(with_late, items)
    gathered = (
        result.reshape(blocks_here, GROUP, BS, HD)
        .transpose(0, 2, 1, 3)
        .reshape(span, 1, GROUP * HD)
    )
    returned = lax.all_to_all(
        as_sent(gathered), "uly", split_axis=0, concat_axis=1, tiled=True
    ).astype(gathered.dtype)
    return returned.reshape(tok, kv_heads * GROUP * HD)


def solution(mesh):
    placed = (P(("blk", "uly"), None), P(("blk", "uly"), None), P(("blk", "uly"), None), P())
    return jax.shard_map(
        local, mesh=mesh, in_specs=placed, out_specs=P(("blk", "uly"), None), check_vma=False
    )
```

profile of v0, /device:TPU:1, one launch (start us, length us, event | category | flops | bytes accessed | tf_op | source)
XLA Modules:
  0.0 395.0 jit_solution(4061454726626957303)
XLA Ops:
  2.3 18.8 %all_to_all.75 = bf16[128,8,256]{0,2,1:T(8,128)(2,1)S(1)} all-to-all(bf16[128,8,256]{0,2,1:T(8,128)(2,1)S(1)} %pad_maximum_fusion), channel_id=1, replica_groups=mesh['blk'=64,'uly'=8] {'uly'}, dimensions={1} | all-to-all | bytes 1048576 | tf_op jit(solution)/shard_map/all_to_all | solution.py:28
  22.2 14.8 %all-to-all-start.2 = ((bf16[1,2,64,8,256]{4,3,1,0,2:T(8,128)(2,1)}), bf16[1,2,64,8,256]{4,3,1,0,2:T(8,128)(2,1)S(1)}, u32[]{:S(2)}, u32[]{:S(2)}) async-start(bf16[1,2,64,8,256]{4,3,1,0,2:T(8,128)(2,1)} %copy.54), calls=%async_computation.2 | async-start | bytes 1048576 | tf_op jit(solution)/shard_map/all_to_all | solution.py:33
  36.9 1.6 copy.68
  38.5 27.6 %all-to-all-done.2 = bf16[1,2,64,8,256]{4,3,1,0,2:T(8,128)(2,1)S(1)} async-done(((bf16[1,2,64,8,256]{4,3,1,0,2:T(8,128)(2,1)}), bf16[1,2,64,8,256]{4,3,1,0,2:T(8,128)(2,1)S(1)}, u32[]{:S(2)}, u32[]{:S(2)}) %all-to-all-start.2) | async-done | bytes 524320 | tf_op jit(solution)/shard_map/all_to_all | solution.py:33
  66.1 8.8 %all-to-all-start = ((bf16[128,8,1024]{2,0,1:T(8,128)(2,1)}), bf16[128,8,1024]{2,0,1:T(8,128)(2,1)}, u32[]{:S(2)}, u32[]{:S(2)}) async-start(bf16[128,8,1024]{2,0,1:T(8,128)(2,1)} %bitcast.66), calls=%async_computation | async-start | bytes 4194304 | tf_op jit(solution)/shard_map/all_to_all | solution.py:27
  75.2 1.7 gather_fusion
  77.0 24.4 %all-to-all-done = bf16[128,8,1024]{2,0,1:T(8,128)(2,1)} async-done(((bf16[128,8,1024]{2,0,1:T(8,128)(2,1)}), bf16[128,8,1024]{2,0,1:T(8,128)(2,1)}, u32[]{:S(2)}, u32[]{:S(2)}) %all-to-all-start) | async-done | bytes 2097184 | tf_op jit(solution)/shard_map/all_to_all | solution.py:27
  101.4 5.6 %all-to-all-start.3 = ((bf16[64,4,1,8,256]{4,3,1,2,0:T(8,128)(2,1)}), bf16[64,4,1,8,256]{4,3,1,2,0:T(8,128)(2,1)S(1)}, u32[]{:S(2)}, u32[]{:S(2)}) async-start(bf16[64,4,1,8,256]{4,3,1,2,0:T(8,128)(2,1)} %bitcast.92), calls=%async_computation.3 | async-start | bytes 2097152 | tf_op jit(solution)/shard_map/all_to_all | solution.py:95
  107.2 2.2 copy.65
  109.4 1.7 copy.58
  111.2 47.3 %all-to-all-done.3 = bf16[64,4,1,8,256]{4,3,1,2,0:T(8,128)(2,1)S(1)} async-done(((bf16[64,4,1,8,256]{4,3,1,2,0:T(8,128)(2,1)}), bf16[64,4,1,8,256]{4,3,1,2,0:T(8,128)(2,1)S(1)}, u32[]{:S(2)}, u32[]{:S(2)}) %all-to-all-start.3) | async-done | bytes 1048608 | tf_op jit(solution)/shard_map/all_to_all | solution.py:95
  158.5 161.7 %while.17 = (s32[]{:T(128)}, bf16[16,512,128]{2,1,0:T(8,128)(2,1)}, s32[16]{0:T(128)S(1)}, bf16[2,512,8,128]{3,1,2,0:T(8,128)(2,1)}, bf16[2,512,256]{2,1,0:T(8,1...) while((s32[]{:T(128)}, bf16[16,512,128]{2,1,0:T(8,128)(2,1)}, ...), condition=%wide.region_5.6_spmd.clone, body=%wide.region_0.5_spmd.clone.sunk | while | flops 410714144 | bytes 12750314 | solution.py:101
  162.3 1.2 broadcast_select_fusion.2
  163.6 1.4 fusion.48
  172.4 1.2 broadcast_select_fusion.2
  173.7 1.4 fusion.48
  175.1 1.2 fusion.49
  182.5 1.2 broadcast_select_fusion.2
  183.8 1.4 fusion.48
  185.2 1.2 fusion.49
  192.6 1.2 broadcast_select_fusion.2
  193.9 1.4 fusion.48
  195.3 1.2 fusion.49
  202.7 1.2 broadcast_select_fusion.2
  204.0 1.4 fusion.48
  205.4 1.2 fusion.49
  212.8 1.2 broadcast_select_fusion.2
  214.1 1.4 fusion.48
  215.5 1.2 fusion.49
  222.9 1.2 broadcast_select_fusion.2
  224.2 1.4 fusion.48
  225.6 1.2 fusion.49
  233.0 1.2 broadcast_select_fusion.2
  234.3 1.4 fusion.48
  235.8 1.2 fusion.49
  243.1 1.2 broadcast_select_fusion.2
  244.4 1.4 fusion.48
  245.9 1.2 fusion.49
  253.2 1.2 broadcast_select_fusion.2
  254.5 1.4 fusion.48
  256.0 1.2 fusion.49
  263.3 1.2 broadcast_select_fusion.2
  264.6 1.4 fusion.48
  266.1 1.2 fusion.49
  274.7 1.4 fusion.48
  276.2 1.2 fusion.49
  284.8 1.4 fusion.48
  286.3 1.2 fusion.49
  294.9 1.4 fusion.48
  296.4 1.2 fusion.49
  305.0 1.4 fusion.48
  306.5 1.2 fusion.49
  313.8 1.2 broadcast_select_fusion.2
  315.1 1.4 fusion.48
  316.6 1.2 fusion.49
  320.2 2.9 copy.69
  323.2 6.2 %reshape.271 = bf16[1024,1,1024]{2,1,0:T(2,128)(2,1)} reshape(bf16[2,512,8,128]{3,2,1,0:T(8,128)(2,1)S(1)} %bitcast.87) | data formatting | bytes 4194304 | tf_op jit(solution)/shard_map/reshape | solution.py:105
  329.9 12.8 %reduce.2 = bf16[1024,1024]{1,0:T(8,128)(2,1)S(1)} reduce(bf16[1024,1,1024]{2,1,0:T(2,128)(2,1)} %reshape.271, bf16[]{:T(256)} %broadcast.234), dimensions={1}, to_apply=%reshape.271.reduce_sub_computation | reduce | bytes 4194306 | tf_op jit(solution)/shard_map/reshape | solution.py:105
  342.7 3.8 reshape.272
  346.5 34.7 %all_to_all.76 = bf16[8,2,65536]{2,1,0:T(2,128)(2,1)S(1)} all-to-all(bf16[8,2,65536]{2,1,0:T(2,128)(2,1)} %reshape.272), channel_id=1, replica_groups=mesh['blk'=64,'uly'=8] {'uly'}, dimensions={0} | all-to-all | bytes 4194304 | tf_op jit(solution)/shard_map/all_to_all | solution.py:107
  381.2 4.4 %reshape.273 = bf16[1024,1,1024]{2,1,0:T(2,128)(2,1)} reshape(bf16[8,2,65536]{2,1,0:T(2,128)(2,1)S(1)} %all_to_all.76) | data formatting | bytes 4194304
  385.6 3.0 copy.63
  388.6 2.4 copy.61
  391.0 4.1 %copy.62 = bf16[128,8192]{1,0:T(8,128)(2,1)} copy(bf16[128,8192]{0,1:T(8,128)(2,1)} %bitcast.90) | data formatting | bytes 4194304 | tf_op jit(solution)/shard_map/reshape | solution.py:110
  (205 shorter events, 69.1 us)
Async XLA Ops:
  0.0 74.9 %copy-start = (s32[128,8,2]{0,2,1:T(2,128)S(1)}, s32[128,8,2]{0,2,1:T(2,128)}, u32[]{:S(2)}) copy-start(s32[128,8,2]{0,2,1:T(2,128)} %param.11) | copy-start | bytes 24580
  2.3 34.6 %copy-start.1 = (bf16[128,8192]{1,0:T(8,128)(2,1)S(1)}, bf16[128,8192]{1,0:T(8,128)(2,1)}, u32[]{:S(2)}) copy-start(bf16[128,8192]{1,0:T(8,128)(2,1)} %param.8) | copy-start | bytes 6291460
  22.2 43.9 %all-to-all-start.2 = ((bf16[1,2,64,8,256]{4,3,1,0,2:T(8,128)(2,1)}), bf16[1,2,64,8,256]{4,3,1,0,2:T(8,128)(2,1)S(1)}, u32[]{:S(2)}, u32[]{:S(2)}) async-start(bf16[1,2,64,8,256]{4,3,1,0,2:T(8,128)(2,1)} %copy.54), calls=%async_computation.2 | async-start | bytes 1048576 | tf_op jit(solution)/shard_map/all_to_all | solution.py:33
  66.1 35.3 %all-to-all-start = ((bf16[128,8,1024]{2,0,1:T(8,128)(2,1)}), bf16[128,8,1024]{2,0,1:T(8,128)(2,1)}, u32[]{:S(2)}, u32[]{:S(2)}) async-start(bf16[128,8,1024]{2,0,1:T(8,128)(2,1)} %bitcast.66), calls=%async_computation | async-start | bytes 4194304 | tf_op jit(solution)/shard_map/all_to_all | solution.py:27
  101.4 57.1 %all-to-all-start.3 = ((bf16[64,4,1,8,256]{4,3,1,2,0:T(8,128)(2,1)}), bf16[64,4,1,8,256]{4,3,1,2,0:T(8,128)(2,1)S(1)}, u32[]{:S(2)}, u32[]{:S(2)}) async-start(bf16[64,4,1,8,256]{4,3,1,2,0:T(8,128)(2,1)} %bitcast.92), calls=%async_computation.3 | async-start | bytes 2097152 | tf_op jit(solution)/shard_map/all_to_all | solution.py:95
  111.2 47.3 %copy-start.2 = (pred[1024]{0:T(1024)(128)(4,1)S(1)}, pred[1024]{0:T(1024)(128)(4,1)}, u32[]{:S(2)}) copy-start(pred[1024]{0:T(1024)(128)(4,1)} %constant.393) | copy-start | bytes 3076
where the time goes:
time: 397 us; the launch traced here: 395 us
  waiting for transfers between devices  99.3 us (25%)
  matrix products  68.3 us (17%)
  local copies, waits for them, and re-layouts  58.5 us (15%)
  blocking collectives  53.5 us (13%)
  other arithmetic  45.2 us (11%)
  loops' own time  41 us (10%)
  starting transfers between devices  29.2 us (7%)
    all_to_all x1, waiting for transfers between devices, local(): lax.all_to_all(request, 'blk', split_axis=0, concat_axis=2, tiled=True)  47.3 us
    another operation x1, loops' own time, local(): result = lax.map(with_late, items)  41 us
    all_to_all x1, blocking collectives, local(): lax.all_to_all(as_sent(gathered), 'uly', split_axis=0, concat_axis=1, til...  34.7 us
    all_to_all x1, waiting for transfers between devices, local(): lax.all_to_all(kv_head.reshape(1, blocks_here, blk_count, pieces, 2 * HD)...  27.6 us
    all_to_all x1, waiting for transfers between devices, local(): lax.all_to_all(q_split, 'uly', split_axis=1, concat_axis=0, tiled=True)  24.4 us
    dot_general x16, matrix products, finish(): lax.dot_general(query_rows, routed_kv[:, :HD], contract, preferred_elemen...  22.9 us
    dot_general x16, matrix products, own_part(): lax.dot_general(query_rows, kv_rows[:, :HD], contract, preferred_element_...  19.6 us
    gather x16, other arithmetic, finish(): routed_mask = jnp.repeat(allowed, BS, total_repeat_length=2 * BS)[None, :]  19.6 us
  transfers between devices with their start and end apart: 3, of which 3 were waited for; matrix products, arithmetic and copies ran while one was open for 2% of the time, Pallas kernels for 0%

commit v1 on v0

v1 whole, which is shorter than its diff:
```python
import functools

import jax
import jax.numpy as jnp
from jax import lax
from jax.experimental import pallas as pl
from jax.experimental.pallas import tpu as pltpu
from jax.sharding import PartitionSpec as P

BS = 512
HD = 128
GROUP = 8
LOG2E = 1.4426950408889634
NEG = -3.0e38
MESH = pl.DeviceIdType.MESH


def kernel(
    blk_n, uly_n, x_n,
    q_ref, k_ref, v_ref, chosen_ref,
    out_ref,
    qh, kv, table, stage, routed, own_acc, own_top, outh,
    kv_send, kv_recv, q_send, q_recv, spread_send, spread_recv, ask_send, ask_recv, out_send, out_recv, self_sem,
):
    rank = lax.axis_index("blk")
    head = lax.axis_index("uly")
    tok = q_ref.shape[0]
    width = GROUP * HD
    span = uly_n * tok
    here = span // BS
    per = BS // tok
    rows = 2 * BS // blk_n
    half_g = GROUP // 2
    z_n = blk_n // x_n
    factor = HD ** (-0.5) * LOG2E
    flip = lax.rem(head, 2)

    def blk_peer(i):
        dx = lax.rem(i, x_n)
        k = lax.div(i, x_n)
        step = lax.div(k + 1, 2)
        dz = jnp.where(lax.rem(k, 2) == 1, step, z_n - step)
        z = lax.rem(lax.div(rank, x_n) + dz, z_n)
        x = lax.rem(lax.rem(rank, x_n) + dx, x_n)
        return z * x_n + x

    def uly_peer(i):
        return lax.rem(head + i, uly_n)

    barrier = pltpu.get_barrier_semaphore()

    def greet_uly(i, c):
        pl.semaphore_signal(barrier, inc=1, device_id=(rank, uly_peer(i)), device_id_type=MESH)
        return c

    def greet_blk(i, c):
        pl.semaphore_signal(barrier, inc=1, device_id=(blk_peer(i), head), device_id_type=MESH)
        return c

    lax.fori_loop(1, uly_n, greet_uly, 0)
    lax.fori_loop(1, blk_n, greet_blk, 0)
    pl.semaphore_wait(barrier, uly_n + blk_n - 2)

    my_block = lax.div(head, per)
    my_row = pl.multiple_of(lax.rem(head, per) * tok, tok)
    my_rows = pl.ds(my_row, tok)
    my_rows_v = pl.ds(pl.multiple_of(my_row + BS, tok), tok)

    def send_kv(i, c):
        p = uly_peer(i)
        cols = pl.ds(pl.multiple_of(p * HD, HD), HD)
        for src, dst_rows in ((k_ref, my_rows), (v_ref, my_rows_v)):
            pltpu.make_async_remote_copy(
                src.at[:, cols], kv.at[my_block, dst_rows, :], kv_send, kv_recv,
                device_id=(rank, p), device_id_type=MESH,
            ).start()
        return c

    lax.fori_loop(1, uly_n, send_kv, 0)
    own_cols = pl.ds(pl.multiple_of(head * HD, HD), HD)
    own_k = pltpu.make_async_copy(k_ref.at[:, own_cols], kv.at[my_block, my_rows, :], self_sem.at[0])
    own_v = pltpu.make_async_copy(v_ref.at[:, own_cols], kv.at[my_block, my_rows_v, :], self_sem.at[1])
    own_k.start()
    own_v.start()

    def send_q(i, c):
        p = uly_peer(i)
        pltpu.make_async_remote_copy(
            q_ref.at[:, pl.ds(pl.multiple_of(p * width, width), width)],
            qh.at[pl.ds(pl.multiple_of(head * tok, tok), tok), :],
            q_send, q_recv, device_id=(rank, p), device_id_type=MESH,
        ).start()
        return c

    lax.fori_loop(1, uly_n, send_q, 0)
    own_q = pltpu.make_async_copy(
        q_ref.at[:, pl.ds(pl.multiple_of(head * width, width), width)],
        qh.at[pl.ds(pl.multiple_of(head * tok, tok), tok), :], self_sem.at[2])
    own_q.start()

    def wait_bytes(ref, sem):
        pltpu.make_async_copy(ref, ref, sem).wait()

    own_k.wait()
    own_v.wait()
    kv_part = kv.at[:, pl.ds(0, 2 * BS * (uly_n - 1) // uly_n), :]
    wait_bytes(kv_part, kv_recv)

    def send_spread(i, c):
        p = blk_peer(i)
        pltpu.make_async_remote_copy(
            kv.at[:, pl.ds(pl.multiple_of(p * rows, rows), rows), :],
            table.at[pl.ds(rank * here, here)],
            spread_send, spread_recv, device_id=(p, head), device_id_type=MESH,
        ).start()
        return c

    lax.fori_loop(1, blk_n, send_spread, 0)
    table[pl.ds(rank * here, here)] = kv[:, pl.ds(pl.multiple_of(rank * rows, rows), rows), :]
    spread_part = table.at[pl.ds(0, here * (blk_n - 1))]
    wait_bytes(spread_part, spread_recv)

    my_share = pl.ds(pl.multiple_of(rank * rows, rows), rows)

    def pick(half, p):
        block = p * here + lax.rem(half + flip, 2)
        for s in range(2):
            stage[half, p, s] = table[chosen_ref[(block * uly_n + head) * 2 + s]]

    def send_ask(n, c):
        half = lax.div(n, blk_n - 1)
        p = blk_peer(lax.rem(n, blk_n - 1) + 1)
        pick(half, p)
        pltpu.make_async_remote_copy(
            stage.at[half, p], routed.at[half, :, my_share, :],
            ask_send, ask_recv.at[half], device_id=(p, head), device_id_type=MESH,
        ).start()
        return c

    lax.fori_loop(0, here * (blk_n - 1), send_ask, 0)
    for half in range(here):
        pick(half, rank)
        routed[half, :, my_share, :] = stage[half, rank]

    own_q.wait()
    wait_bytes(qh.at[pl.ds(0, span - tok), :], q_recv)

    def queries(row, gh):
        return jnp.concatenate(
            [qh[pl.ds(row, tok), pl.ds(pl.multiple_of((gh * half_g + g) * HD, HD), HD)] for g in range(half_g)], axis=0)

    contract = (((1,), (1,)), ((), ()))
    ones = jnp.ones((BS, HD), jnp.bfloat16)

    def own_step(i, c):
        b = lax.div(i, 2)
        gh = lax.rem(i, 2)
        for part in range(per):
            q = queries(pl.multiple_of(b * BS + part * tok, tok), gh)
            n = (part + 1) * tok
            scores = lax.dot_general(q, kv[b, 0:n, :], contract, preferred_element_type=jnp.float32)
            r = lax.rem(lax.broadcasted_iota(jnp.int32, (half_g * tok, tok), 0), tok)
            k = lax.broadcasted_iota(jnp.int32, (half_g * tok, tok), 1)
            diag = jnp.where(k <= r, scores[:, n - tok:], -jnp.inf)
            if part:
                scores = jnp.concatenate([scores[:, : n - tok], diag], axis=1)
            else:
                scores = diag
            top = jnp.max(scores, axis=1, keepdims=True)
            weights = jnp.exp2(scores * factor - top * factor).astype(jnp.bfloat16)
            v1 = jnp.concatenate([kv[b, BS:BS + n, :], ones[:n]], axis=1)
            own_acc[b, part, gh] = jnp.dot(weights, v1, preferred_element_type=jnp.float32)
            own_top[b, part, gh] = jnp.broadcast_to(top, (half_g * tok, HD))
        return c

    lax.fori_loop(0, here * 2, own_step, 0)

    def routed_step(n, c):
        half = lax.div(n, per)
        b = lax.rem(half + flip, 2)
        part = lax.rem(n + lax.div(head, 2), per)

        @pl.when(lax.rem(n, per) == 0)
        def _():
            wait_bytes(spread_part, ask_recv.at[half])

        block = rank * here + b
        usable = [chosen_ref[(block * uly_n + head) * 2 + s] < block for s in range(2)]
        row = pl.multiple_of(b * BS + part * tok, tok)

        def group_step(gh, c):
            q = queries(row, gh)
            before = own_top[b, part, gh][:, 0:1]
            scores = [
                lax.dot_general(q, routed[half, s, 0:BS, :], contract, preferred_element_type=jnp.float32)
                for s in range(2)
            ]
            top = before
            for s in range(2):
                top = jnp.maximum(top, jnp.where(usable[s], jnp.max(scores[s], axis=1, keepdims=True), NEG))
            acc = own_acc[b, part, gh] * jnp.exp2((before - top) * factor)
            for s in range(2):
                shift = jnp.where(usable[s], top * factor, jnp.inf)
                weights = jnp.exp2(scores[s] * factor - shift).astype(jnp.bfloat16)
                v1 = jnp.concatenate([routed[half, s, BS:, :], ones], axis=1)
                acc = acc + jnp.dot(weights, v1, preferred_element_type=jnp.float32)
            result = (acc[:, :HD] / acc[:, HD:]).astype(jnp.bfloat16)
            for g in range(half_g):
                outh[pl.ds(row, tok), pl.ds(pl.multiple_of((gh * half_g + g) * HD, HD), HD)] = (
                    result[g * tok:(g + 1) * tok])
            return c

        lax.fori_loop(0, 2, group_step, 0)
        p = b * per + part
        src = outh.at[pl.ds(row, tok), :]
        dst = out_ref.at[:, pl.ds(pl.multiple_of(head * width, width), width)]

        @pl.when(p != head)
        def _():
            pltpu.make_async_remote_copy(
                src, dst, out_send, out_recv, device_id=(rank, p), device_id_type=MESH).start()

        @pl.when(p == head)
        def _():
            pltpu.make_async_copy(src, dst, self_sem.at[3]).start()

        return c

    lax.fori_loop(0, here * per, routed_step, 0)

    pltpu.make_async_copy(
        outh.at[pl.ds(0, tok), :], out_ref.at[:, pl.ds(0, width)], self_sem.at[3]).wait()
    wait_bytes(kv_part, kv_send)
    wait_bytes(qh.at[pl.ds(0, span - tok), :], q_send)
    wait_bytes(spread_part, spread_send)
    wait_bytes(stage.at[:, pl.ds(0, blk_n - 1)], ask_send)
    wait_bytes(qh.at[pl.ds(0, span - tok), :], out_send)
    wait_bytes(qh.at[pl.ds(0, span - tok), :], out_recv)


def solution(mesh):
    blk_n, uly_n = mesh.shape["blk"], mesh.shape["uly"]
    x_n = 4 if blk_n % 4 == 0 else 1

    def local(queries, keys, values, chosen):
        tok = queries.shape[0]
        span = tok * uly_n
        here = span // BS
        rows = 2 * BS // blk_n
        per = BS // tok
        bf = jnp.bfloat16
        any_spec = pl.BlockSpec(memory_space=pl.ANY)
        dma = pltpu.SemaphoreType.DMA
        return pl.pallas_call(
            functools.partial(kernel, blk_n, uly_n, x_n),
            out_shape=jax.ShapeDtypeStruct(queries.shape, bf),
            in_specs=[any_spec, any_spec, any_spec, pl.BlockSpec(memory_space=pltpu.SMEM)],
            out_specs=any_spec,
            scratch_shapes=[
                pltpu.VMEM((span, GROUP * HD), bf),
                pltpu.VMEM((here, 2 * BS, HD), bf),
                pltpu.VMEM((blk_n * here, rows, HD), bf),
                pltpu.VMEM((here, blk_n, 2, rows, HD), bf),
                pltpu.VMEM((here, 2, 2 * BS, HD), bf),
                pltpu.VMEM((here, per, 2, GROUP // 2 * tok, 2 * HD), jnp.float32),
                pltpu.VMEM((here, per, 2, GROUP // 2 * tok, HD), jnp.float32),
                pltpu.VMEM((span, GROUP * HD), bf),
                dma, dma, dma, dma, dma, dma, dma, dma((here,)), dma, dma, dma((4,)),
            ],
            compiler_params=pltpu.CompilerParams(
                collective_id=0, has_side_effects=True, vmem_limit_bytes=56 * 2**20),
        )(queries, keys, values, chosen.reshape(-1))

    placed = P(("blk", "uly"), None)
    return jax.shard_map(
        local, mesh=mesh, in_specs=(placed, placed, placed, P()), out_specs=placed, check_vma=False)
```

time: 397 us -> 131 us (0.33)
  Pallas kernels: 0 us -> 126 us
  waiting for transfers between devices: 99.3 us -> 0 us
  matrix products: 68.3 us -> 0 us
  local copies, waits for them, and re-layouts: 58.5 us -> 4.9 us
  blocking collectives: 53.5 us -> 0 us
  other arithmetic: 45.2 us -> 0 us
  loops' own time: 41 us -> 0 us
  starting transfers between devices: 29.2 us -> 0 us
    pallas_call x0 -> x1, Pallas kernels: none -> 126 us  [local(): pl.pallas_call(functools.partial(kernel, blk_n, uly_n, x_n), out_shape=ja...]
    all_to_all x3 -> x0, waiting for transfers between devices: 99.3 us -> none  [the longest x1 47.3 us: local(): lax.all_to_all(request, 'blk', split_axis=0, concat_axis=2, tiled=True)]
    dot_general x64 -> x0, matrix products: 68.3 us -> none  [the longest x16 22.9 us: finish(): lax.dot_general(query_rows, routed_kv[:, :HD], contract, preferred_elemen...]
    all_to_all x2 -> x0, blocking collectives: 53.5 us -> none  [the longest x1 34.7 us: local(): lax.all_to_all(as_sent(gathered), 'uly', split_axis=0, concat_axis=1, til...]
    another operation x1 -> x0, loops' own time: 41 us -> none  [local(): result = lax.map(with_late, items)]
    all_to_all x3 -> x0, starting transfers between devices: 29.2 us -> none  [the longest x1 14.8 us: local(): lax.all_to_all(kv_head.reshape(1, blocks_here, blk_count, pieces, 2 * HD)...]
    gather x17 -> x0, other arithmetic: 19.6 us -> none  [the longest x16 19.6 us: finish(): routed_mask = jnp.repeat(allowed, BS, total_repeat_length=2 * BS)[None, :]]
    reshape x7 -> x1, local copies, waits for them, and re-layouts: 16.2 us -> 0.87 us  [local(): chosen.reshape(-1)]
  transfers between devices with their start and end apart: 3 -> 0, of which waited for: 3 -> 0; matrix products, arithmetic and copies ran while one was open for 2% -> 0% of each run, Pallas kernels for 0% -> 0%
where the time goes in v1:
time: 131 us
  Pallas kernels  126 us (96%)
  local copies, waits for them, and re-layouts  4.9 us (4%)
    pallas_call x1, Pallas kernels, local(): pl.pallas_call(functools.partial(kernel, blk_n, uly_n, x_n), out_shape=ja...  126 us
    unnamed x2, local copies, waits for them, and re-layouts  4.04 us

profile of v1, /device:TPU:1, one launch (start us, length us, event | category | flops | bytes accessed | tf_op | source)
XLA Modules:
  0.0 130.8 jit_solution(16392580507298971394)
XLA Ops:
  0.0 0.9 copy.5
  0.9 0.9 reshape.3.chosen_ref
  1.8 125.9 %shard_map.46 = bf16[128,8192]{1,0:T(8,128)(2,1)} custom-call(bf16[128,8192]{1,0:T(8,128)(2,1)} %q_ref.1, bf16[128,1024]{1,0:T(8,128)(2,1)} %k_ref.1, bf16[128,1024]{1,0:T(8,128)(2,1)} %v_ref.1, s32[2048]{0:T(1024)} %reshape.3.chosen_ref), custom_call_target="tpu_custom_call" | custom-call | tf_op jit(solution)/shard_map/pallas_call | solution.py:254
  127.7 3.1 %copy.7 = bf16[128,8192]{1,0:T(8,128)(2,1)} copy(bf16[128,8192]{1,0:T(8,128)(2,1)} %shard_map.46) | data formatting | bytes 4194304

commit v2 on v1

--- a/solution.py
+++ b/solution.py
@@ -20,7 +20,7 @@
     q_ref, k_ref, v_ref, chosen_ref,
     out_ref,
     qh, kv, table, stage, routed, own_acc, own_top, outh,
-    kv_send, kv_recv, q_send, q_recv, spread_send, spread_recv, ask_send, ask_recv, out_send, out_recv, self_sem,
+    kv_send, kv_recv, q_send, q_recv, spread_send, spread_recv, ask_send, ask_recv, out_send, out_recv, self_sem, turn,
 ):
     rank = lax.axis_index("blk")
     head = lax.axis_index("uly")
@@ -33,9 +33,14 @@
     half_g = GROUP // 2
     z_n = blk_n // x_n
     factor = HD ** (-0.5) * LOG2E
-    flip = lax.rem(head, 2)
+    home = lax.div(head, per)
+    seat = lax.rem(head, per)
+
+    def own_last(half):
+        return jnp.where(half == here - 1, home, here - 1 - home)
 
     def blk_peer(i):
+        i = lax.rem(blk_n - i, blk_n)
         dx = lax.rem(i, x_n)
         k = lax.div(i, x_n)
         step = lax.div(k + 1, 2)
@@ -61,22 +66,26 @@
     lax.fori_loop(1, blk_n, greet_blk, 0)
     pl.semaphore_wait(barrier, uly_n + blk_n - 2)
 
-    my_block = lax.div(head, per)
-    my_row = pl.multiple_of(lax.rem(head, per) * tok, tok)
+    my_block = home
+    my_row = pl.multiple_of(seat * tok, tok)
     my_rows = pl.ds(my_row, tok)
     my_rows_v = pl.ds(pl.multiple_of(my_row + BS, tok), tok)
 
     def send_kv(i, c):
-        p = uly_peer(i)
+        p = 2 * lax.rem(lax.div(head, 2) + lax.rem(i, uly_n // 2), uly_n // 2) + lax.div(i, uly_n // 2)
         cols = pl.ds(pl.multiple_of(p * HD, HD), HD)
-        for src, dst_rows in ((k_ref, my_rows), (v_ref, my_rows_v)):
-            pltpu.make_async_remote_copy(
-                src.at[:, cols], kv.at[my_block, dst_rows, :], kv_send, kv_recv,
-                device_id=(rank, p), device_id_type=MESH,
-            ).start()
-        return c
-
-    lax.fori_loop(1, uly_n, send_kv, 0)
+
+        @pl.when(p != head)
+        def _():
+            for src, dst_rows in ((k_ref, my_rows), (v_ref, my_rows_v)):
+                pltpu.make_async_remote_copy(
+                    src.at[:, cols], kv.at[my_block, dst_rows, :], kv_send, kv_recv,
+                    device_id=(rank, p), device_id_type=MESH,
+                ).start()
+
+        return c
+
+    lax.fori_loop(0, uly_n, send_kv, 0)
     own_cols = pl.ds(pl.multiple_of(head * HD, HD), HD)
     own_k = pltpu.make_async_copy(k_ref.at[:, own_cols], kv.at[my_block, my_rows, :], self_sem.at[0])
     own_v = pltpu.make_async_copy(v_ref.at[:, own_cols], kv.at[my_block, my_rows_v, :], self_sem.at[1])
@@ -106,6 +115,10 @@
     kv_part = kv.at[:, pl.ds(0, 2 * BS * (uly_n - 1) // uly_n), :]
     wait_bytes(kv_part, kv_recv)
 
+    @pl.when(lax.rem(head, 2) == 1)
+    def _():
+        pl.semaphore_wait(turn, 1)
+
     def send_spread(i, c):
         p = blk_peer(i)
         pltpu.make_async_remote_copy(
@@ -118,29 +131,36 @@
     lax.fori_loop(1, blk_n, send_spread, 0)
     table[pl.ds(rank * here, here)] = kv[:, pl.ds(pl.multiple_of(rank * rows, rows), rows), :]
     spread_part = table.at[pl.ds(0, here * (blk_n - 1))]
+
+    @pl.when(lax.rem(head, 2) == 0)
+    def _():
+        wait_bytes(spread_part, spread_send)
+        pl.semaphore_signal(turn, inc=1, device_id=(rank, head + 1), device_id_type=MESH)
+
     wait_bytes(spread_part, spread_recv)
 
     my_share = pl.ds(pl.multiple_of(rank * rows, rows), rows)
 
-    def pick(half, p):
-        block = p * here + lax.rem(half + flip, 2)
+    def pick(half, p, s):
+        block = p * here + own_last(half)
+        stage[half, s, p] = table[chosen_ref[head, s, block]]
+
+    def send_ask(n, c):
+        part = lax.div(n, blk_n - 1)
+        half, s = lax.div(part, 2), lax.rem(part, 2)
+        p = blk_peer(lax.rem(n, blk_n - 1) + 1)
+        pick(half, p, s)
+        pltpu.make_async_remote_copy(
+            stage.at[half, s, p], routed.at[half, s, my_share, :],
+            ask_send, ask_recv.at[half, s], device_id=(p, head), device_id_type=MESH,
+        ).start()
+        return c
+
+    lax.fori_loop(0, 2 * here * (blk_n - 1), send_ask, 0)
+    for half in range(here):
         for s in range(2):
-            stage[half, p, s] = table[chosen_ref[(block * uly_n + head) * 2 + s]]
-
-    def send_ask(n, c):
-        half = lax.div(n, blk_n - 1)
-        p = blk_peer(lax.rem(n, blk_n - 1) + 1)
-        pick(half, p)
-        pltpu.make_async_remote_copy(
-            stage.at[half, p], routed.at[half, :, my_share, :],
-            ask_send, ask_recv.at[half], device_id=(p, head), device_id_type=MESH,
-        ).start()
-        return c
-
-    lax.fori_loop(0, here * (blk_n - 1), send_ask, 0)
-    for half in range(here):
-        pick(half, rank)
-        routed[half, :, my_share, :] = stage[half, rank]
+            pick(half, rank, s)
+            routed[half, s, my_share, :] = stage[half, s, rank]
 
     own_q.wait()
     wait_bytes(qh.at[pl.ds(0, span - tok), :], q_recv)
@@ -176,64 +196,95 @@
     lax.fori_loop(0, here * 2, own_step, 0)
 
     def routed_step(n, c):
-        half = lax.div(n, per)
-        b = lax.rem(half + flip, 2)
-        part = lax.rem(n + lax.div(head, 2), per)
+        quarter = lax.div(n, per)
+        half, s = lax.div(quarter, 2), lax.rem(quarter, 2)
+        b = own_last(half)
+        turn_of = lax.rem(n, per)
+        part = jnp.where(turn_of == 0, lax.rem(seat + 2, per), jnp.where(
+            turn_of == 1, per - 1 - seat, jnp.where(turn_of == 2, seat + 1 - 2 * lax.rem(seat, 2), seat)))
 
         @pl.when(lax.rem(n, per) == 0)
         def _():
-            wait_bytes(spread_part, ask_recv.at[half])
+            wait_bytes(table.at[pl.ds(0, blk_n - 1)], ask_recv.at[half, s])
 
         block = rank * here + b
-        usable = [chosen_ref[(block * uly_n + head) * 2 + s] < block for s in range(2)]
+        usable = chosen_ref[head, s, block] < block
         row = pl.multiple_of(b * BS + part * tok, tok)
 
-        def group_step(gh, c):
-            q = queries(row, gh)
-            before = own_top[b, part, gh][:, 0:1]
-            scores = [
-                lax.dot_general(q, routed[half, s, 0:BS, :], contract, preferred_element_type=jnp.float32)
-                for s in range(2)
-            ]
-            top = before
-            for s in range(2):
-                top = jnp.maximum(top, jnp.where(usable[s], jnp.max(scores[s], axis=1, keepdims=True), NEG))
-            acc = own_acc[b, part, gh] * jnp.exp2((before - top) * factor)
-            for s in range(2):
-                shift = jnp.where(usable[s], top * factor, jnp.inf)
-                weights = jnp.exp2(scores[s] * factor - shift).astype(jnp.bfloat16)
-                v1 = jnp.concatenate([routed[half, s, BS:, :], ones], axis=1)
-                acc = acc + jnp.dot(weights, v1, preferred_element_type=jnp.float32)
-            result = (acc[:, :HD] / acc[:, HD:]).astype(jnp.bfloat16)
-            for g in range(half_g):
-                outh[pl.ds(row, tok), pl.ds(pl.multiple_of((gh * half_g + g) * HD, HD), HD)] = (
-                    result[g * tok:(g + 1) * tok])
-            return c
-
-        lax.fori_loop(0, 2, group_step, 0)
+        v1 = jnp.concatenate([routed[half, s, BS:, :], ones], axis=1)
+        chains = [(j // 1, (j % 1) * 4 * tok, j * 4) for j in range(2)]
+
+        def heads(g0):
+            return jnp.concatenate([qh[pl.ds(row, tok), (g0 + g) * HD:(g0 + g + 1) * HD] for g in range(4)], axis=0)
+
+        def score(chain):
+            return lax.dot_general(heads(chain[2]), routed[half, s, 0:BS, :], contract, preferred_element_type=jnp.float32)
+
+        def one(chain, scores):
+            gh, r0, g0 = chain
+            rr = slice(r0, r0 + 4 * tok)
+            before = own_top[b, part, gh, rr]
+            peak = jnp.broadcast_to(jnp.max(scores, axis=1, keepdims=True), before.shape)
+            top = jnp.maximum(before, jnp.where(usable, peak, NEG))
+            shift = jnp.where(usable, top * factor, jnp.inf)
+            weights = jnp.exp2(scores * factor - jnp.concatenate([shift] * (BS // HD), axis=1)).astype(jnp.bfloat16)
+            alpha = jnp.exp2((before - top) * factor)
+            acc = own_acc[b, part, gh, rr] * jnp.concatenate([alpha, alpha], axis=1)
+            return acc + jnp.dot(weights, v1, preferred_element_type=jnp.float32), top
+
+        def run():
+            out = []
+            if True:
+                nxt = score(chains[0])
+                for i, ch in enumerate(chains):
+                    cur = nxt
+                    if i + 1 < len(chains):
+                        nxt = score(chains[i + 1])
+                    out.append((ch, *one(ch, cur)))
+            else:
+                out = [(ch, *one(ch, score(ch))) for ch in chains]
+            return out
+
+        @pl.when(s == 0)
+        def _():
+            for (gh, r0, g0), acc, top in run():
+                own_acc[b, part, gh, r0:r0 + 4 * tok] = acc
+                own_top[b, part, gh, r0:r0 + 4 * tok] = top
+
+        @pl.when(s == 1)
+        def _():
+            for (gh, r0, g0), acc, top in run():
+                result = (acc[:, :HD] / acc[:, HD:]).astype(jnp.bfloat16)
+                for g in range(4):
+                    outh[pl.ds(row, tok), (g0 + g) * HD:(g0 + g + 1) * HD] = result[g * tok:(g + 1) * tok]
+
         p = b * per + part
         src = outh.at[pl.ds(row, tok), :]
         dst = out_ref.at[:, pl.ds(pl.multiple_of(head * width, width), width)]
 
-        @pl.when(p != head)
+        @pl.when((s == 1) & (p != head))
         def _():
             pltpu.make_async_remote_copy(
                 src, dst, out_send, out_recv, device_id=(rank, p), device_id_type=MESH).start()
 
-        @pl.when(p == head)
+        @pl.when((s == 1) & (p == head))
         def _():
             pltpu.make_async_copy(src, dst, self_sem.at[3]).start()
 
         return c
 
-    lax.fori_loop(0, here * per, routed_step, 0)
+    lax.fori_loop(0, 2 * here * per, routed_step, 0)
 
     pltpu.make_async_copy(
         outh.at[pl.ds(0, tok), :], out_ref.at[:, pl.ds(0, width)], self_sem.at[3]).wait()
     wait_bytes(kv_part, kv_send)
     wait_bytes(qh.at[pl.ds(0, span - tok), :], q_send)
-    wait_bytes(spread_part, spread_send)
-    wait_bytes(stage.at[:, pl.ds(0, blk_n - 1)], ask_send)
+
+    @pl.when(lax.rem(head, 2) == 1)
+    def _():
+        wait_bytes(spread_part, spread_send)
+
+    wait_bytes(stage.at[:, :, pl.ds(0, blk_n - 1)], ask_send)
     wait_bytes(qh.at[pl.ds(0, span - tok), :], out_send)
     wait_bytes(qh.at[pl.ds(0, span - tok), :], out_recv)
 
@@ -250,26 +301,28 @@
         per = BS // tok
         bf = jnp.bfloat16
         any_spec = pl.BlockSpec(memory_space=pl.ANY)
+        hbm_spec = pl.BlockSpec(memory_space=pltpu.HBM)
         dma = pltpu.SemaphoreType.DMA
         return pl.pallas_call(
             functools.partial(kernel, blk_n, uly_n, x_n),
             out_shape=jax.ShapeDtypeStruct(queries.shape, bf),
-            in_specs=[any_spec, any_spec, any_spec, pl.BlockSpec(memory_space=pltpu.SMEM)],
+            in_specs=[hbm_spec, hbm_spec, hbm_spec, pl.BlockSpec(memory_space=pltpu.SMEM)],
             out_specs=any_spec,
             scratch_shapes=[
                 pltpu.VMEM((span, GROUP * HD), bf),
                 pltpu.VMEM((here, 2 * BS, HD), bf),
                 pltpu.VMEM((blk_n * here, rows, HD), bf),
-                pltpu.VMEM((here, blk_n, 2, rows, HD), bf),
+                pltpu.VMEM((here, 2, blk_n, rows, HD), bf),
                 pltpu.VMEM((here, 2, 2 * BS, HD), bf),
                 pltpu.VMEM((here, per, 2, GROUP // 2 * tok, 2 * HD), jnp.float32),
                 pltpu.VMEM((here, per, 2, GROUP // 2 * tok, HD), jnp.float32),
                 pltpu.VMEM((span, GROUP * HD), bf),
-                dma, dma, dma, dma, dma, dma, dma, dma((here,)), dma, dma, dma((4,)),
+                dma, dma, dma, dma, dma, dma, dma, dma((here, 2)), dma, dma, dma((4,)),
+                pltpu.SemaphoreType.REGULAR,
             ],
             compiler_params=pltpu.CompilerParams(
-                collective_id=0, has_side_effects=True, vmem_limit_bytes=56 * 2**20),
-        )(queries, keys, values, chosen.reshape(-1))
+                collective_id=0, has_side_effects=True, vmem_limit_bytes=36 * 2**20),
+        )(*[pltpu.with_memory_space_constraint(a, pltpu.HBM) for a in (queries, keys, values)], chosen.transpose(1, 2, 0))
 
     placed = P(("blk", "uly"), None)
     return jax.shard_map(

time: 131 us -> 109 us (0.83)
  Pallas kernels: 126 us -> 106 us
  local copies, waits for them, and re-layouts: 4.9 us -> 2.02 us
    pallas_call x1, Pallas kernels: 126 us -> 106 us  [local(): pl.pallas_call(functools.partial(kernel, blk_n, uly_n, x_n), out_shape=ja...]
    unnamed x2 -> x3, local copies, waits for them, and re-layouts: 4.04 us -> 2.02 us
where the time goes in v2:
time: 109 us; the launch traced here: 108 us
  Pallas kernels  106 us (97%)
  local copies, waits for them, and re-layouts  2.02 us (2%)
    pallas_call x1, Pallas kernels, local(): pl.pallas_call(functools.partial(kernel, blk_n, uly_n, x_n), out_shape=ja...  106 us

profile of v2, /device:TPU:1, one launch (start us, length us, event | category | flops | bytes accessed | tf_op | source)
XLA Modules:
  0.0 107.8 jit_solution(14280932428701813996)
XLA Ops:
  0.0 0.0 copy-start
  0.0 0.7 copy-done
  0.7 105.8 %shard_map.46 = bf16[128,8192]{1,0:T(8,128)(2,1)S(1)} custom-call(bf16[128,8192]{1,0:T(8,128)(2,1)} %q_ref.1, bf16[128,1024]{1,0:T(8,128)(2,1)} %k_ref.1, bf16[128,1024]{1,0:T(8,128)(2,1)} %v_ref.1, s32[8,2,128]{2,1,0:T(2,128)S(1)} %bitcast.1), custom_call_target="tpu_custom_call" | custom-call | tf_op jit(solution)/shard_map/pallas_call | solution.py:306
  106.5 1.3 %copy.6 = bf16[128,8192]{1,0:T(8,128)(2,1)} copy(bf16[128,8192]{1,0:T(8,128)(2,1)S(1)} %shard_map.46) | data formatting | bytes 4194304
Async XLA Ops:
  0.0 0.7 copy-start

commit v3 on v2

--- a/solution.py
+++ b/solution.py
@@ -10,6 +10,7 @@
 BS = 512
 HD = 128
 GROUP = 8
+EARLY = 4
 LOG2E = 1.4426950408889634
 NEG = -3.0e38
 MESH = pl.DeviceIdType.MESH
@@ -17,8 +18,9 @@
 
 def kernel(
     blk_n, uly_n, x_n,
-    q_ref, k_ref, v_ref, chosen_ref,
+    q_ref, k_ref, v_ref, ids_ref,
     out_ref,
+    chosen_ref,
     qh, kv, table, stage, routed, own_acc, own_top, outh,
     kv_send, kv_recv, q_send, q_recv, spread_send, spread_recv, ask_send, ask_recv, out_send, out_recv, self_sem, turn,
 ):
@@ -39,31 +41,42 @@
     def own_last(half):
         return jnp.where(half == here - 1, home, here - 1 - home)
 
-    def blk_peer(i):
-        i = lax.rem(blk_n - i, blk_n)
-        dx = lax.rem(i, x_n)
-        k = lax.div(i, x_n)
-        step = lax.div(k + 1, 2)
-        dz = jnp.where(lax.rem(k, 2) == 1, step, z_n - step)
-        z = lax.rem(lax.div(rank, x_n) + dz, z_n)
-        x = lax.rem(lax.rem(rank, x_n) + dx, x_n)
-        return z * x_n + x
+    my_z, my_x = lax.div(rank, x_n), lax.rem(rank, x_n)
+    xs = [lax.rem(my_x + dx, x_n) for dx in range(x_n)]
+
+    def share_of(p):
+        return pl.ds(pl.multiple_of(lax.rem(p, 2) * BS + lax.div(p, 2) * rows, rows), rows)
+
+    def for_blk(action, columns=xs, last=xs[1:]):
+        def at(i, c):
+            k = z_n - 1 - i
+            odd = lax.rem(k, 2)
+            step = lax.div(k + 1, 2)
+            z = lax.rem(my_z + z_n + step * (2 * odd - 1), z_n)
+            action(i, [z * x_n + x for x in columns])
+            return c
+
+        lax.fori_loop(0, z_n - 1, at, 0)
+        action(z_n - 1, [my_z * x_n + x for x in last])
 
     def uly_peer(i):
         return lax.rem(head + i, uly_n)
 
+    ids = pltpu.make_async_copy(ids_ref, chosen_ref, self_sem.at[4])
+    ids.start()
+
     barrier = pltpu.get_barrier_semaphore()
 
     def greet_uly(i, c):
         pl.semaphore_signal(barrier, inc=1, device_id=(rank, uly_peer(i)), device_id_type=MESH)
         return c
 
-    def greet_blk(i, c):
-        pl.semaphore_signal(barrier, inc=1, device_id=(blk_peer(i), head), device_id_type=MESH)
-        return c
+    def greet_blk(i, peers):
+        for p in peers:
+            pl.semaphore_signal(barrier, inc=1, device_id=(p, head), device_id_type=MESH)
 
     lax.fori_loop(1, uly_n, greet_uly, 0)
-    lax.fori_loop(1, blk_n, greet_blk, 0)
+    for_blk(greet_blk)
     pl.semaphore_wait(barrier, uly_n + blk_n - 2)
 
     my_block = home
@@ -71,21 +84,26 @@
     my_rows = pl.ds(my_row, tok)
     my_rows_v = pl.ds(pl.multiple_of(my_row + BS, tok), tok)
 
-    def send_kv(i, c):
-        p = 2 * lax.rem(lax.div(head, 2) + lax.rem(i, uly_n // 2), uly_n // 2) + lax.div(i, uly_n // 2)
-        cols = pl.ds(pl.multiple_of(p * HD, HD), HD)
-
-        @pl.when(p != head)
-        def _():
-            for src, dst_rows in ((k_ref, my_rows), (v_ref, my_rows_v)):
+    def send_kv(parity, kind):
+        src, dst_rows = ((k_ref, my_rows), (v_ref, my_rows_v))[kind]
+
+        def at(i, c):
+            p = 2 * lax.rem(lax.div(head, 2) + i, uly_n // 2) + parity
+
+            @pl.when(p != head)
+            def _():
                 pltpu.make_async_remote_copy(
-                    src.at[:, cols], kv.at[my_block, dst_rows, :], kv_send, kv_recv,
-                    device_id=(rank, p), device_id_type=MESH,
+                    src.at[:, pl.ds(pl.multiple_of(p * HD, HD), HD)], kv.at[my_block, dst_rows, :],
+                    kv_send, kv_recv.at[kind], device_id=(rank, p), device_id_type=MESH,
                 ).start()
 
-        return c
-
-    lax.fori_loop(0, uly_n, send_kv, 0)
+            return c
+
+        lax.fori_loop(0, uly_n // 2, at, 0)
+
+    for parity in range(2):
+        for kind in range(2):
+            send_kv(parity, kind)
     own_cols = pl.ds(pl.multiple_of(head * HD, HD), HD)
     own_k = pltpu.make_async_copy(k_ref.at[:, own_cols], kv.at[my_block, my_rows, :], self_sem.at[0])
     own_v = pltpu.make_async_copy(v_ref.at[:, own_cols], kv.at[my_block, my_rows_v, :], self_sem.at[1])
@@ -110,53 +128,65 @@
     def wait_bytes(ref, sem):
         pltpu.make_async_copy(ref, ref, sem).wait()
 
-    own_k.wait()
-    own_v.wait()
     kv_part = kv.at[:, pl.ds(0, 2 * BS * (uly_n - 1) // uly_n), :]
-    wait_bytes(kv_part, kv_recv)
+    half_part = kv.at[:, pl.ds(0, BS * (uly_n - 1) // uly_n), :]
 
     @pl.when(lax.rem(head, 2) == 1)
     def _():
         pl.semaphore_wait(turn, 1)
 
-    def send_spread(i, c):
-        p = blk_peer(i)
-        pltpu.make_async_remote_copy(
-            kv.at[:, pl.ds(pl.multiple_of(p * rows, rows), rows), :],
-            table.at[pl.ds(rank * here, here)],
-            spread_send, spread_recv, device_id=(p, head), device_id_type=MESH,
-        ).start()
-        return c
-
-    lax.fori_loop(1, blk_n, send_spread, 0)
-    table[pl.ds(rank * here, here)] = kv[:, pl.ds(pl.multiple_of(rank * rows, rows), rows), :]
+    def spread(kind, early):
+        def send(i, peers):
+            for p in peers:
+                @pl.when(p != rank)
+                def _():
+                    pltpu.make_async_remote_copy(
+                        kv.at[:, share_of(p), :], table.at[pl.ds(rank * here, here)],
+                        spread_send.at[jnp.where(i < early, 0, 1)], spread_recv,
+                        device_id=(p, head), device_id_type=MESH,
+                    ).start()
+
+        for_blk(send, range(kind, x_n, 2), range(kind, x_n, 2))
+
+    own_k.wait()
+    wait_bytes(half_part, kv_recv.at[0])
+    spread(0, z_n - 1)
+    own_v.wait()
+    wait_bytes(half_part, kv_recv.at[1])
+    spread(1, EARLY)
+    table[pl.ds(rank * here, here)] = kv[:, share_of(rank), :]
     spread_part = table.at[pl.ds(0, here * (blk_n - 1))]
 
     @pl.when(lax.rem(head, 2) == 0)
     def _():
-        wait_bytes(spread_part, spread_send)
+        wait_bytes(table.at[pl.ds(0, here * 2 * (z_n - 1 + EARLY))], spread_send.at[0])
         pl.semaphore_signal(turn, inc=1, device_id=(rank, head + 1), device_id_type=MESH)
 
     wait_bytes(spread_part, spread_recv)
 
-    my_share = pl.ds(pl.multiple_of(rank * rows, rows), rows)
+    ids.wait()
+    my_share = share_of(rank)
 
     def pick(half, p, s):
         block = p * here + own_last(half)
         stage[half, s, p] = table[chosen_ref[head, s, block]]
 
-    def send_ask(n, c):
-        part = lax.div(n, blk_n - 1)
-        half, s = lax.div(part, 2), lax.rem(part, 2)
-        p = blk_peer(lax.rem(n, blk_n - 1) + 1)
-        pick(half, p, s)
-        pltpu.make_async_remote_copy(
-            stage.at[half, s, p], routed.at[half, s, my_share, :],
-            ask_send, ask_recv.at[half, s], device_id=(p, head), device_id_type=MESH,
-        ).start()
-        return c
-
-    lax.fori_loop(0, 2 * here * (blk_n - 1), send_ask, 0)
+    def send_asks(n, c):
+        half, s = lax.div(n, 2), lax.rem(n, 2)
+
+        def send_ask(i, peers):
+            for p in peers:
+                pick(half, p, s)
+            for p in peers:
+                pltpu.make_async_remote_copy(
+                    stage.at[half, s, p], routed.at[half, s, my_share, :],
+                    ask_send, ask_recv.at[half, s], device_id=(p, head), device_id_type=MESH,
+                ).start()
+
+        for_blk(send_ask)
+        return c
+
+    lax.fori_loop(0, 2 * here, send_asks, 0)
     for half in range(here):
         for s in range(2):
             pick(half, rank, s)
@@ -282,7 +312,9 @@
 
     @pl.when(lax.rem(head, 2) == 1)
     def _():
-        wait_bytes(spread_part, spread_send)
+        wait_bytes(table.at[pl.ds(0, here * 2 * (z_n - 1 + EARLY))], spread_send.at[0])
+
+    wait_bytes(table.at[pl.ds(0, here * (blk_n - 1 - 2 * (z_n - 1 + EARLY)))], spread_send.at[1])
 
     wait_bytes(stage.at[:, :, pl.ds(0, blk_n - 1)], ask_send)
     wait_bytes(qh.at[pl.ds(0, span - tok), :], out_send)
@@ -306,9 +338,10 @@
         return pl.pallas_call(
             functools.partial(kernel, blk_n, uly_n, x_n),
             out_shape=jax.ShapeDtypeStruct(queries.shape, bf),
-            in_specs=[hbm_spec, hbm_spec, hbm_spec, pl.BlockSpec(memory_space=pltpu.SMEM)],
+            in_specs=[hbm_spec] * 4,
             out_specs=any_spec,
             scratch_shapes=[
+                pltpu.SMEM((chosen.shape[1], chosen.shape[2], chosen.shape[0]), jnp.int32),
                 pltpu.VMEM((span, GROUP * HD), bf),
                 pltpu.VMEM((here, 2 * BS, HD), bf),
                 pltpu.VMEM((blk_n * here, rows, HD), bf),
@@ -317,12 +350,12 @@
                 pltpu.VMEM((here, per, 2, GROUP // 2 * tok, 2 * HD), jnp.float32),
                 pltpu.VMEM((here, per, 2, GROUP // 2 * tok, HD), jnp.float32),
                 pltpu.VMEM((span, GROUP * HD), bf),
-                dma, dma, dma, dma, dma, dma, dma, dma((here, 2)), dma, dma, dma((4,)),
+                dma, dma((2,)), dma, dma, dma((2,)), dma, dma, dma((here, 2)), dma, dma, dma((5,)),
                 pltpu.SemaphoreType.REGULAR,
             ],
             compiler_params=pltpu.CompilerParams(
                 collective_id=0, has_side_effects=True, vmem_limit_bytes=36 * 2**20),
-        )(*[pltpu.with_memory_space_constraint(a, pltpu.HBM) for a in (queries, keys, values)], chosen.transpose(1, 2, 0))
+        )(*[pltpu.with_memory_space_constraint(a, pltpu.HBM) for a in (queries, keys, values, chosen.transpose(1, 2, 0))])
 
     placed = P(("blk", "uly"), None)
     return jax.shard_map(

time: 109 us -> 106 us (0.972)
    pallas_call x1, Pallas kernels: 106 us -> 105 us  [local(): pl.pallas_call(functools.partial(kernel, blk_n, uly_n, x_n), out_shape=ja...]
where the time goes in v3:
time: 106 us
  Pallas kernels  105 us (99%)
  local copies, waits for them, and re-layouts  1.32 us (1%)
    pallas_call x1, Pallas kernels, local(): pl.pallas_call(functools.partial(kernel, blk_n, uly_n, x_n), out_shape=ja...  105 us

profile of v3, /device:TPU:1, one launch (start us, length us, event | category | flops | bytes accessed | tf_op | source)
XLA Modules:
  0.0 105.8 jit_solution(8033389167003769851)
XLA Ops:
  0.0 104.5 %shard_map.46 = bf16[128,8192]{1,0:T(8,128)(2,1)S(1)} custom-call(bf16[128,8192]{1,0:T(8,128)(2,1)} %q_ref.1, bf16[128,1024]{1,0:T(8,128)(2,1)} %k_ref.1, bf16[128,1024]{1,0:T(8,128)(2,1)} %v_ref.1, s32[8,2,128]{2,1,0:T(2,128)} %bitcast.1), custom_call_target="tpu_custom_call" | custom-call | tf_op jit(solution)/shard_map/pallas_call | solution.py:338
  104.5 1.3 %copy.6 = bf16[128,8192]{1,0:T(8,128)(2,1)} copy(bf16[128,8192]{1,0:T(8,128)(2,1)S(1)} %shard_map.46) | data formatting | bytes 4194304

commit v4 on v3

--- a/solution.py
+++ b/solution.py
@@ -22,7 +22,7 @@
     out_ref,
     chosen_ref,
     qh, kv, table, stage, routed, own_acc, own_top, outh,
-    kv_send, kv_recv, q_send, q_recv, spread_send, spread_recv, ask_send, ask_recv, out_send, out_recv, self_sem, turn,
+    kv_send, kv_recv, q_send, q_recv, spread_send, spread_recv, ask_send, ask_recv, out_send, out_recv, self_sem, turn, heard,
 ):
     rank = lax.axis_index("blk")
     head = lax.axis_index("uly")
@@ -45,19 +45,20 @@
     xs = [lax.rem(my_x + dx, x_n) for dx in range(x_n)]
 
     def share_of(p):
-        return pl.ds(pl.multiple_of(lax.rem(p, 2) * BS + lax.div(p, 2) * rows, rows), rows)
-
-    def for_blk(action, columns=xs, last=xs[1:]):
+        kind = lax.rem(lax.div(p, x_n) + p, 2)
+        return pl.ds(pl.multiple_of(kind * BS + lax.div(p, 2) * rows, rows), rows)
+
+    def for_blk(action, columns=lambda z: xs, last=lambda z: xs[1:]):
         def at(i, c):
             k = z_n - 1 - i
             odd = lax.rem(k, 2)
             step = lax.div(k + 1, 2)
             z = lax.rem(my_z + z_n + step * (2 * odd - 1), z_n)
-            action(i, [z * x_n + x for x in columns])
+            action(i, [z * x_n + x for x in columns(z)])
             return c
 
         lax.fori_loop(0, z_n - 1, at, 0)
-        action(z_n - 1, [my_z * x_n + x for x in last])
+        action(z_n - 1, [my_z * x_n + x for x in last(my_z)])
 
     def uly_peer(i):
         return lax.rem(head + i, uly_n)
@@ -76,8 +77,8 @@
             pl.semaphore_signal(barrier, inc=1, device_id=(p, head), device_id_type=MESH)
 
     lax.fori_loop(1, uly_n, greet_uly, 0)
-    for_blk(greet_blk)
-    pl.semaphore_wait(barrier, uly_n + blk_n - 2)
+    for_blk(greet_blk, lambda z: [my_x])
+    pl.semaphore_wait(barrier, uly_n + z_n + x_n - 3)
 
     my_block = home
     my_row = pl.multiple_of(seat * tok, tok)
@@ -109,6 +110,9 @@
     own_v = pltpu.make_async_copy(v_ref.at[:, own_cols], kv.at[my_block, my_rows_v, :], self_sem.at[1])
     own_k.start()
     own_v.start()
+
+    for x in xs[1:]:
+        pl.semaphore_signal(heard, inc=1, device_id=(my_z * x_n + x, head), device_id_type=MESH)
 
     def send_q(i, c):
         p = uly_peer(i)
@@ -146,8 +150,13 @@
                         device_id=(p, head), device_id_type=MESH,
                     ).start()
 
-        for_blk(send, range(kind, x_n, 2), range(kind, x_n, 2))
-
+        def columns(z):
+            first = my_x + lax.rem(kind + z + my_x, 2)
+            return [lax.rem(first + dx, x_n) for dx in range(0, x_n, 2)]
+
+        for_blk(send, columns, columns)
+
+    pl.semaphore_wait(heard, x_n - 1)
     own_k.wait()
     wait_bytes(half_part, kv_recv.at[0])
     spread(0, z_n - 1)
@@ -351,7 +360,7 @@
                 pltpu.VMEM((here, per, 2, GROUP // 2 * tok, HD), jnp.float32),
                 pltpu.VMEM((span, GROUP * HD), bf),
                 dma, dma((2,)), dma, dma, dma((2,)), dma, dma, dma((here, 2)), dma, dma, dma((5,)),
-                pltpu.SemaphoreType.REGULAR,
+                pltpu.SemaphoreType.REGULAR, pltpu.SemaphoreType.REGULAR,
             ],
             compiler_params=pltpu.CompilerParams(
                 collective_id=0, has_side_effects=True, vmem_limit_bytes=36 * 2**20),

time: 106 us -> 105 us (level)
  no operation moved by 1% of the time
where the time goes in v4:
time: 105 us
  Pallas kernels  104 us (99%)
  local copies, waits for them, and re-layouts  1.32 us (1%)
    pallas_call x1, Pallas kernels, local(): pl.pallas_call(functools.partial(kernel, blk_n, uly_n, x_n), out_shape=ja...  104 us

profile of v4, /device:TPU:1, one launch (start us, length us, event | category | flops | bytes accessed | tf_op | source)
XLA Modules:
  0.0 105.3 jit_solution(3824150246004144929)
XLA Ops:
  0.0 104.0 %shard_map.46 = bf16[128,8192]{1,0:T(8,128)(2,1)S(1)} custom-call(bf16[128,8192]{1,0:T(8,128)(2,1)} %q_ref.1, bf16[128,1024]{1,0:T(8,128)(2,1)} %k_ref.1, bf16[128,1024]{1,0:T(8,128)(2,1)} %v_ref.1, s32[8,2,128]{2,1,0:T(2,128)} %bitcast.1), custom_call_target="tpu_custom_call" | custom-call | tf_op jit(solution)/shard_map/pallas_call | solution.py:347
  104.0 1.3 %copy.6 = bf16[128,8192]{1,0:T(8,128)(2,1)} copy(bf16[128,8192]{1,0:T(8,128)(2,1)S(1)} %shard_map.46) | data formatting | bytes 4194304

commit v5 on v4

--- a/solution.py
+++ b/solution.py
@@ -77,7 +77,13 @@
             pl.semaphore_signal(barrier, inc=1, device_id=(p, head), device_id_type=MESH)
 
     lax.fori_loop(1, uly_n, greet_uly, 0)
-    for_blk(greet_blk, lambda z: [my_x])
+    def greet_z(k, c):
+        step = lax.div(k + 1, 2) * (2 * lax.rem(k, 2) - 1)
+        greet_blk(k, [lax.rem(my_z + z_n + step, z_n) * x_n + my_x])
+        return c
+
+    greet_blk(0, [my_z * x_n + x for x in xs[1:]])
+    lax.fori_loop(1, z_n, greet_z, 0)
     pl.semaphore_wait(barrier, uly_n + z_n + x_n - 3)
 
     my_block = home

time: 105 us -> 106 us (level)
  no operation moved by 1% of the time
where the time goes in v5:
time: 106 us
  Pallas kernels  104 us (98%)
  local copies, waits for them, and re-layouts  1.32 us (1%)
    pallas_call x1, Pallas kernels, local(): pl.pallas_call(functools.partial(kernel, blk_n, uly_n, x_n), out_shape=ja...  104 us

profile of v5, /device:TPU:1, one launch (start us, length us, event | category | flops | bytes accessed | tf_op | source)
XLA Modules:
  0.0 105.5 jit_solution(11962837982497197595)
XLA Ops:
  0.0 104.2 %shard_map.46 = bf16[128,8192]{1,0:T(8,128)(2,1)S(1)} custom-call(bf16[128,8192]{1,0:T(8,128)(2,1)} %q_ref.1, bf16[128,1024]{1,0:T(8,128)(2,1)} %k_ref.1, bf16[128,1024]{1,0:T(8,128)(2,1)} %v_ref.1, s32[8,2,128]{2,1,0:T(2,128)} %bitcast.1), custom_call_target="tpu_custom_call" | custom-call | tf_op jit(solution)/shard_map/pallas_call | solution.py:353
  104.2 1.3 %copy.6 = bf16[128,8192]{1,0:T(8,128)(2,1)} copy(bf16[128,8192]{1,0:T(8,128)(2,1)S(1)} %shard_map.46) | data formatting | bytes 4194304
